TPU v7x, 32 devices: a whole 2x2x4 slice. The times are simulated.
32 devices in a mesh: dp: 4 (over y, x), context: 8 (over z, core).
Axes of the slice: x: 2, y: 2, z: 4, core: 2. Of those that a mesh axis runs over, the one named last changes fastest.
Arguments:
- projected: bfloat16 [4096, 6144], P(('dp', 'context')), may hold values from -6 to 6
- short_taps: float32 [3, 6144], replicated, may hold values from -4 to 4
- long_filter: float32 [2048, 1024], P('context'), may hold values from -1.5 to 1.5
- skip_gain: float32 [2048], P('context'), may hold values from -4 to 4
- out_proj: bfloat16 [2048, 2048], P('dp'), may hold values from -0.125 to 0.125
- cotangent: bfloat16 [4096, 2048], P(('dp', 'context')), may hold values from -25 to 25
Outputs:
- grad_inputs: bfloat16 [4096, 6144], P(('dp', 'context'))
- grad_taps: float32 [3, 6144], replicated
- grad_filter: float32 [2048, 1024], P('context', 'dp')
- grad_skip: float32 [2048], P('context')
- grad_proj: float32 [2048, 2048], P(('dp', 'context'))
All inputs are finite; a program needn't handle non-finite values.
Results may differ from a plain program's by a relative error of at most 0.012.
Values may be sent and summed in bfloat16 or wider, within the bound.
No kernel may reach another device: no remote copies, remote signals or barrier semaphores. Data moves between devices by JAX's collectives and lax.ppermute only.
A program may use at most 128 MiB of HBM per device.

v0:
```python
import math
import jax
import jax.numpy as jnp
from jax import lax
from jax.sharding import PartitionSpec as P

PRECISE = lax.Precision.HIGH


def passed_along(value, axis, steps):
    count = lax.axis_size(axis)
    initial, last = (max(0, -steps), min(count, count - steps))
    return lax.ppermute(value, axis, [(source, source + steps) for source in range(initial, last)])


def angle_table(first_count, second_count, period):
    first_idx = lax.broadcasted_iota(jnp.int32, (first_count, second_count), 0)
    second_idx = lax.broadcasted_iota(jnp.int32, (first_count, second_count), 1)
    phases = first_idx * second_idx % period
    angles = phases.astype(jnp.float32) * (-2.0 * math.pi / period)
    return (jnp.cos(angles), jnp.sin(angles))


def make_tables(seq_len):
    radix_size = min(128, seq_len)
    blocks = 2 * seq_len // radix_size
    half_blocks = blocks // 2
    outer_re, outer_im = angle_table(blocks, blocks, blocks)
    twist = angle_table(blocks, radix_size, blocks * radix_size)
    inner_re, inner_im = angle_table(radix_size, radix_size, radix_size)
    first_table = jnp.concatenate([outer_re[:, :half_blocks], outer_im[:, :half_blocks]], 0)
    inner_fwd = jnp.concatenate(
        [jnp.concatenate([inner_re, inner_im], 1), jnp.concatenate([-inner_im, inner_re], 1)], 0
    )
    inner_back = jnp.concatenate(
        [jnp.concatenate([inner_re, -inner_im], 1), jnp.concatenate([inner_im, inner_re], 1)], 0
    )
    last_table = jnp.concatenate([outer_re[:half_blocks, :], outer_im[:half_blocks, :]], 1)
    return (first_table, twist, inner_fwd, inner_back, last_table)


def forward_spectrum(signal, tables):
    first_table, (twist_re, twist_im), inner_fwd, inner_back, last_table = tables
    blocks = twist_re.shape[0]
    radix_size = twist_re.shape[1]
    shaped = signal.reshape(signal.shape[0], blocks // 2, radix_size)
    first = jnp.einsum("kn,cnm->ckm", first_table, shaped, precision=PRECISE)
    first_re = first[:, :blocks]
    first_im = first[:, blocks:]
    turned = jnp.concatenate(
        [first_re * twist_re - first_im * twist_im, first_re * twist_im + first_im * twist_re], 2
    )
    return jnp.einsum("ckn,nm->ckm", turned, inner_fwd, precision=PRECISE)


def spectral_product(left, right, conjugate_left):
    width = left.shape[2] // 2
    left_re, left_im = (left[:, :, :width], left[:, :, width:])
    right_re, right_im = (right[:, :, :width], right[:, :, width:])
    if conjugate_left:
        return jnp.concatenate(
            [left_re * right_re + left_im * right_im, left_re * right_im - left_im * right_re], 2
        )
    return jnp.concatenate(
        [left_re * right_re - left_im * right_im, left_re * right_im + left_im * right_re], 2
    )


def inverse_real(spectrum, tables):
    first_table, (twist_re, twist_im), inner_fwd, inner_back, last_table = tables
    blocks = twist_re.shape[0]
    radix_size = twist_re.shape[1]
    undo = jnp.einsum("ckn,nm->ckm", spectrum, inner_back, precision=PRECISE)
    undo_re = undo[:, :, :radix_size]
    undo_im = undo[:, :, radix_size:]
    back = jnp.concatenate(
        [undo_re * twist_re + undo_im * twist_im, undo_im * twist_re - undo_re * twist_im], 1
    )
    result = jnp.einsum("nk,ckm->cnm", last_table, back, precision=PRECISE)
    return result.reshape(spectrum.shape[0], blocks // 2 * radix_size) / (blocks * radix_size)


def body(projected, short_taps, long_filter, skip_gain, out_proj, cotangent):
    tok_rows = projected.shape[0]
    chan_all = projected.shape[1] // 3
    prev_rows = passed_along(projected[tok_rows - 2 :], "context", 1)
    extended = jnp.concatenate([prev_rows, projected], 0).astype(jnp.float32)
    current = extended[2:]
    once_back = extended[1 : tok_rows + 1]
    twice_back = extended[:tok_rows]
    mixed = short_taps[0] * current + short_taps[1] * once_back + short_taps[2] * twice_back
    query = mixed[:, :chan_all].astype(jnp.bfloat16)
    keyed = mixed[:, chan_all : 2 * chan_all].astype(jnp.bfloat16)
    valued = mixed[:, 2 * chan_all :].astype(jnp.bfloat16)
    product = (keyed.astype(jnp.float32) * valued.astype(jnp.float32)).astype(jnp.bfloat16)
    product_chan = lax.all_to_all(product.T, "context", split_axis=0, concat_axis=1, tiled=True)
    seq_len = product_chan.shape[1]
    tables = make_tables(seq_len)
    prod_f = product_chan.astype(jnp.float32)
    filter_spec = forward_spectrum(long_filter, tables)
    prod_spec = forward_spectrum(prod_f, tables)
    long_chan = (
        inverse_real(spectral_product(filter_spec, prod_spec, False), tables)
        + skip_gain[:, None] * prod_f
    )
    long_tok = lax.all_to_all(
        long_chan.astype(jnp.bfloat16), "context", split_axis=1, concat_axis=0, tiled=True
    ).T
    gate = (query.astype(jnp.float32) * long_tok.astype(jnp.float32)).astype(jnp.bfloat16)
    grad_gate = lax.dot_general(
        cotangent,
        lax.all_gather(out_proj, "dp", axis=0, tiled=True),
        (((1,), (1,)), ((), ())),
        preferred_element_type=jnp.float32,
    ).astype(jnp.bfloat16)
    grad_rows = lax.psum_scatter(
        lax.dot_general(
            gate, cotangent, (((0,), (0,)), ((), ())), preferred_element_type=jnp.float32
        ),
        ("dp", "context"),
        scatter_dimension=0,
        tiled=True,
    )
    grad_query = grad_gate.astype(jnp.float32) * long_tok.astype(jnp.float32)
    grad_long = (grad_gate.astype(jnp.float32) * query.astype(jnp.float32)).astype(jnp.bfloat16)
    grad_chan = lax.all_to_all(
        grad_long.T, "context", split_axis=0, concat_axis=1, tiled=True
    ).astype(jnp.float32)
    grad_spec = forward_spectrum(grad_chan, tables)
    back_chan = (
        inverse_real(spectral_product(filter_spec, grad_spec, True), tables)
        + skip_gain[:, None] * grad_chan
    )
    filter_local = inverse_real(spectral_product(prod_spec, grad_spec, True), tables)
    grad_product = lax.all_to_all(
        back_chan.astype(jnp.bfloat16), "context", split_axis=1, concat_axis=0, tiled=True
    ).T
    scale_factor = 1.0 / math.sqrt(seq_len * lax.axis_size("dp"))
    grad_filter = (
        lax.psum_scatter(filter_local, "dp", scatter_dimension=1, tiled=True) * scale_factor
    )
    grad_skip = lax.psum(jnp.sum(grad_chan * prod_f, axis=1), "dp") * scale_factor
    grad_key = grad_product.astype(jnp.float32) * valued.astype(jnp.float32)
    grad_value = grad_product.astype(jnp.float32) * keyed.astype(jnp.float32)
    grad_mixed = jnp.concatenate([grad_query, grad_key, grad_value], 1)
    next_rows = passed_along(grad_mixed[:2].astype(jnp.bfloat16), "context", -1).astype(jnp.float32)
    grad_ext = jnp.concatenate([grad_mixed, next_rows], 0)
    grad_inputs = (
        short_taps[0] * grad_ext[:tok_rows]
        + short_taps[1] * grad_ext[1 : tok_rows + 1]
        + short_taps[2] * grad_ext[2:]
    ).astype(jnp.bfloat16)
    taps_terms = jnp.stack(
        [
            jnp.sum(grad_mixed * current, 0),
            jnp.sum(grad_mixed * once_back, 0),
            jnp.sum(grad_mixed * twice_back, 0),
        ]
    )
    grad_taps = lax.psum(taps_terms, ("dp", "context")) * scale_factor
    return (grad_inputs, grad_taps, grad_filter, grad_skip, grad_rows * scale_factor)


def solution(mesh):
    placed = (
        P(("dp", "context"), None),
        P(),
        P("context", None),
        P("context"),
        P("dp", None),
        P(("dp", "context"), None),
    )
    return jax.shard_map(
        body,
        mesh=mesh,
        in_specs=placed,
        out_specs=(
            P(("dp", "context"), None),
            P(),
            P("context", "dp"),
            P("context"),
            P(("dp", "context"), None),
        ),
        check_vma=False,
    )
```

profile of v0, /device:TPU:0, one launch (start us, length us, event | category | flops | bytes accessed | tf_op | source)
XLA Modules:
  0.0 625.5 jit_solution(3541810269681701199)
XLA Ops:
  7.2 0.7 all-gather.2.cloned.1.call-update
  7.9 0.9 slice.124
  8.8 2.4 collective-permute-start
  11.2 1.1 fusion.109
  12.9 1.7 copy-done.1
  14.6 1.0 add_convert_fusion
  15.6 84.6 %all-gather.2.cloned.1.call-done = bf16[2048,2048]{1,0:T(8,128)(2,1)} async-done(((bf16[512,2048]{1,0:T(8,128)(2,1)}), bf16[2048,2048]{1,0:T(8,128)(2,1)}) %all-gather.2.cloned.1.call-update) | async-done | bytes 8388624 | tf_op jit(solution)/shard_map/all_gather | solution.py:112
  100.2 6.2 fusion.21
  106.5 1.0 copy-done.11
  107.6 1.0 copy.71
  108.6 4.6 all-to-all-start.2
  113.4 1.4 copy.77
  115.5 3.9 convolution_bitcast_fusion.2
  119.5 9.1 %all-to-all-done.2 = bf16[8,256,128]{2,1,0:T(8,128)(2,1)S(1)} async-done(((bf16[8,256,128]{2,1,0:T(8,128)(2,1)}), bf16[8,256,128]{2,1,0:T(8,128)(2,1)S(1)}, u32[]{:S(2)}, u32[]{:S(2)}) %all-to-all-start.2) | async-done | bytes 524320 | tf_op jit(solution)/shard_map/all_to_all | solution.py:126
  128.6 1.4 convolution_bitcast_fusion
  130.0 1.0 copy-done.7
  131.0 0.9 multiply_subtract_fusion.8
  131.8 0.7 pad_maximum_fusion
  132.6 4.2 fusion.16
  136.8 4.2 fusion.12
  141.0 0.9 multiply_add_fusion.3
  142.0 1.0 copy-done.5
  143.0 2.6 pad_maximum_fusion.4
  145.5 5.5 copy.61
  151.0 4.0 fusion.68
  155.7 3.2 fusion.46
  159.0 17.8 %all_to_all.52 = bf16[256,8,128]{2,0,1:T(8,128)(2,1)S(1)} all-to-all(bf16[256,8,128]{2,0,1:T(8,128)(2,1)S(1)} %copy.52), channel_id=1, replica_groups=mesh['dp'=4,'context'=8] {'context'}, dimensions={1} | all-to-all | bytes 1048576 | tf_op jit(solution)/shard_map/all_to_all | solution.py:135
  176.9 1.3 copy.74
  178.2 2.8 convert_multiply_fusion.5
  181.2 17.8 %all_to_all.53 = bf16[8,256,128]{2,1,0:T(8,128)(2,1)S(1)} all-to-all(bf16[8,256,128]{2,1,0:T(8,128)(2,1)S(1)} %bitcast.96), channel_id=1, replica_groups=mesh['dp'=4,'context'=8] {'context'}, dimensions={0} | all-to-all | bytes 1048576 | tf_op jit(solution)/shard_map/all_to_all | solution.py:96
  199.0 0.8 copy-done.15
  199.8 1.4 convolution_bitcast_fusion.1
  202.0 4.1 fusion.14
  206.1 4.4 multiply_add_fusion.1
  210.5 4.6 pad_maximum_fusion.5
  215.1 5.5 copy.64
  220.6 6.1 fusion.66
  226.8 2.3 pad_maximum_fusion.2
  229.0 5.6 copy.58
  234.7 4.3 fusion.70
  239.0 2.8 multiply_add_fusion
  241.8 3.2 fusion.43
  245.1 17.8 %all_to_all.54 = bf16[256,8,128]{2,0,1:T(8,128)(2,1)S(1)} all-to-all(bf16[256,8,128]{2,0,1:T(8,128)(2,1)S(1)} %copy.43), channel_id=1, replica_groups=mesh['dp'=4,'context'=8] {'context'}, dimensions={1} | all-to-all | bytes 1048576 | tf_op jit(solution)/shard_map/all_to_all | solution.py:106
  262.9 1.1 convert_element_type.197
  263.9 2.6 copy.70
  266.5 1.7 bitcast_multiply_fusion
  268.4 1.3 collective-permute-start.1
  269.7 1.8 collective-permute-done.1
  271.9 1.6 copy-done.2
  273.5 3.0 multiply_reduce_fusion.2
  276.5 0.7 pad_maximum_fusion.12
  277.3 3.5 fusion.22
  280.8 1.2 copy.98
  282.0 9.1 %fusion.53 = f32[2048,2048]{1,0:T(8,128)} fusion(bf16[128,2048]{1,0:T(8,128)(2,1)S(1)} %copy-done, f32[2048,128]{0,1:T(8,128)S(1)} %copy-done.10, bf16[128,6144]{1,0:T(8,128)(2,1)} %copy-done.12), kind=kOutput, calls=%fused_computation.82 | convolution fusion | flops 1074528256 | bytes 18874368 | tf_op jit(solution)/shard_map/dot_general | solution.py:117
  291.2 1.0 copy-done.14
  292.4 1.1 fusion.52
  293.5 8.9 %psum.15 = f32[256]{0:T(256)S(1)} all-reduce(f32[256]{0:T(256)S(1)} %fusion.52), channel_id=1, replica_groups=mesh['dp'=4,'context'=8] {'dp'}, use_global_device_ids=true, to_apply=%region_6.7 | all-reduce | flops 256 | bytes 2048 | tf_op jit(solution)/shard_map/psum | solution.py:142
  302.4 0.6 broadcast_multiply_fusion.3
  303.0 93.5 %all-reduce.2.cloned.1.call-done = f32[3,6144]{1,0:T(4,128)} async-done(((f32[3,6144]{1,0:T(4,128)}), f32[3,6144]{1,0:T(4,128)}) %all-reduce.2.cloned.1.call-update) | async-done | bytes 73744 | tf_op jit(solution)/shard_map/psum | solution.py:160
  396.5 1.6 broadcast_multiply_fusion.2
  398.0 29.9 %reduce-scatter.3.cloned.1.call-done = f32[256,256]{1,0:T(8,128)} async-done(((f32[256,1024]{1,0:T(8,128)}), f32[256,256]{1,0:T(8,128)}) %reduce-scatter.3.cloned.1.call-update) | async-done | bytes 262160 | tf_op jit(solution)/shard_map/reduce_scatter | solution.py:140
  428.0 1.7 broadcast_multiply_fusion.1
  429.6 187.3 %reduce-scatter.5.cloned.1.call-done = f32[64,2048]{1,0:T(8,128)} async-done(((f32[2048,2048]{1,0:T(8,128)}), f32[64,2048]{1,0:T(8,128)}) %reduce-scatter.5.cloned.1.call-update) | async-done | bytes 524304 | tf_op jit(solution)/shard_map/reduce_scatter | solution.py:116
  616.9 1.9 broadcast_multiply_fusion
  (68 shorter events, 4.4 us)
Async XLA Ops:
  7.2 93.1 %copy-start = (bf16[128,2048]{1,0:T(8,128)(2,1)S(1)}, bf16[128,2048]{1,0:T(8,128)(2,1)}, u32[]{:S(2)}) copy-start(bf16[128,2048]{1,0:T(8,128)(2,1)} %param.11) | copy-start | bytes 1572868
  7.2 5.3 copy-start.20
  7.2 93.0 %all-gather.2.cloned.1.call-start = ((), (), s32[]{:S(2)}) async-start(), calls=%async_computation.6 | async-start | bytes 10485760 | tf_op jit(solution)/shard_map/all_gather | solution.py:112
  8.8 3.6 collective-permute-start
  12.9 1.7 copy-start.1
  15.6 90.9 %copy-start.12 = (bf16[128,6144]{1,0:T(8,128)(2,1)}, bf16[128,6144]{1,0:T(8,128)(2,1)S(1)}, u32[]{:S(2)}) copy-start(bf16[128,6144]{1,0:T(8,128)(2,1)S(1)} %add_convert_fusion) | copy-start | bytes 4718596
  106.5 1.0 copy-start.11
  108.6 20.0 %all-to-all-start.2 = ((bf16[8,256,128]{2,1,0:T(8,128)(2,1)}), bf16[8,256,128]{2,1,0:T(8,128)(2,1)S(1)}, u32[]{:S(2)}, u32[]{:S(2)}) async-start(bf16[8,256,128]{2,1,0:T(8,128)(2,1)} %bitcast.17), calls=%async_computation.2 | async-start | bytes 1048576 | tf_op jit(solution)/shard_map/all_to_all | solution.py:126
  113.2 283.3 %all-reduce.2.cloned.1.call-start = ((), (), s32[]{:S(2)}) async-start(), calls=%async_computation.7 | async-start | bytes 196608 | tf_op jit(solution)/shard_map/psum | solution.py:160
  128.6 26.9 %copy-start.13 = (bf16[8,256,128]{2,1,0:T(8,128)(2,1)}, bf16[8,256,128]{2,1,0:T(8,128)(2,1)S(1)}, u32[]{:S(2)}) copy-start(bf16[8,256,128]{2,1,0:T(8,128)(2,1)S(1)} %all-to-all-done.2) | copy-start | bytes 1572868
  128.6 2.4 copy-start.7
  136.8 4.2 copy-start.3
  141.0 1.9 copy-start.5
  155.1 0.7 copy-start.21
  199.0 0.8 copy-start.15
  201.9 4.1 copy-start.4
  202.0 4.1 copy-start.6
  220.6 6.1 copy-start.18
  220.6 6.1 copy-start.19
  234.7 4.3 copy-start.8
  239.0 2.8 copy-start.16
  262.9 5.3 copy-start.9
  268.4 3.1 collective-permute-start.1
  271.5 1.9 copy-start.2
  277.2 150.8 %reduce-scatter.3.cloned.1.call-start = ((), (), s32[]{:S(2)}) async-start(), calls=%async_computation.8 | async-start | bytes 1310720 | tf_op jit(solution)/shard_map/reduce_scatter | solution.py:140
  277.3 4.8 copy-start.10
  282.0 334.9 %reduce-scatter.5.cloned.1.call-start = ((), (), s32[]{:S(2)}) async-start(), calls=%async_computation.9 | async-start | bytes 17301504 | tf_op jit(solution)/shard_map/reduce_scatter | solution.py:116
  291.2 1.0 copy-start.14
  291.2 1.2 copy-start.17
Sparse Core Ops, SparseCore 0:
  9.9 90.2 all-gather.1
  277.3 119.1 all-reduce.1
  399.4 28.5 reduce-scatter.2
  430.2 186.6 reduce-scatter.4
where the time goes:
time: 631 us; the launch traced here: 626 us
  waiting for transfers between devices  407 us (65%)
  blocking collectives  62.2 us (10%)
  matrix products  58.9 us (9%)
  other arithmetic  39.3 us (6%)
  local copies, waits for them, and re-layouts  35.3 us (6%)
  between operations  14.5 us (2%)
  starting transfers between devices  8.42 us (1%)
    reduce_scatter x1, waiting for transfers between devices, body(): lax.psum_scatter(lax.dot_general(gate, cotangent, (((0,), (0,)), ((), ())...  187 us
    psum x1, waiting for transfers between devices, body(): grad_taps = lax.psum(taps_terms, ('dp', 'context')) * scale_factor  93.5 us
    all_gather x1, waiting for transfers between devices, body(): lax.all_gather(out_proj, 'dp', axis=0, tiled=True)  84.6 us
    reduce_scatter x1, waiting for transfers between devices, body(): lax.psum_scatter(filter_local, 'dp', scatter_dimension=1, tiled=True)  29.9 us
    all_to_all x1, blocking collectives, body(): lax.all_to_all(back_chan.astype(jnp.bfloat16), 'context', split_axis=1, c...  17.8 us
    all_to_all x1, blocking collectives, body(): lax.all_to_all(product.T, 'context', split_axis=0, concat_axis=1, tiled=T...  17.8 us
    all_to_all x1, blocking collectives, body(): lax.all_to_all(long_chan.astype(jnp.bfloat16), 'context', split_axis=1, c...  17.8 us
    dot_general x3, matrix products, inverse_real(): undo = jnp.einsum('ckn,nm->ckm', spectrum, inner_back, precision=PRECISE)  14.4 us
  transfers between devices with their start and end apart: 7, of which 6 were waited for; matrix products, arithmetic and copies ran while one was open for 5% of the time, Pallas kernels for 0%

commit v1 on v0

--- a/solution.py
+++ b/solution.py
@@ -93,7 +93,19 @@
     keyed = mixed[:, chan_all : 2 * chan_all].astype(jnp.bfloat16)
     valued = mixed[:, 2 * chan_all :].astype(jnp.bfloat16)
     product = (keyed.astype(jnp.float32) * valued.astype(jnp.float32)).astype(jnp.bfloat16)
-    product_chan = lax.all_to_all(product.T, "context", split_axis=0, concat_axis=1, tiled=True)
+    ways, here = (lax.axis_size("context"), lax.axis_index("context"))
+    width_2 = product.T.shape[0] // ways
+    shape = list(product.T.shape)
+    shape[0] = width_2
+    height = shape[1]
+    shape[1] = height * ways
+    full = jnp.zeros(shape, product.T.dtype)
+    for mask in range(ways):
+        part = lax.dynamic_slice_in_dim(product.T, (here ^ mask) * width_2, width_2, axis=0)
+        if mask:
+            part = lax.ppermute(part, "context", [(d, d ^ mask) for d in range(ways)])
+        full = lax.dynamic_update_slice_in_dim(full, part, (here ^ mask) * height, axis=1)
+    product_chan = full
     seq_len = product_chan.shape[1]
     tables = make_tables(seq_len)
     prod_f = product_chan.astype(jnp.float32)

time: 631 us -> 630 us (level)
  blocking collectives: 62.2 us -> 28.9 us
  waiting for transfers between devices: 407 us -> 428 us
  starting transfers between devices: 8.42 us -> 20.4 us
    all_to_all x2 -> x0, blocking collectives: 35.5 us -> none  [the longest x1 17.8 us: body(): lax.all_to_all(back_chan.astype(jnp.bfloat16), 'context', split_axis=1, c...]
    all_to_all x0 -> x1, waiting for transfers between devices: none -> 13.4 us  [body(): lax.all_to_all(back_chan.astype(jnp.bfloat16), 'context', split_axis=1, c...]
    ppermute x0 -> x7, starting transfers between devices: none -> 8.26 us  [body(): part = lax.ppermute(part, 'context', [(d, d ^ mask) for d in range(ways)])]
  transfers between devices with their start and end apart: 7 -> 15, of which waited for: 6 -> 9; matrix products, arithmetic and copies ran while one was open for 5% -> 5% of each run, Pallas kernels for 0% -> 0%
where the time goes in v1:
time: 630 us; the launch traced here: 624 us
  waiting for transfers between devices  428 us (68%)
  matrix products  57.9 us (9%)
  other arithmetic  37.9 us (6%)
  local copies, waits for them, and re-layouts  36.4 us (6%)
  blocking collectives  28.9 us (5%)
  starting transfers between devices  20.4 us (3%)
  between operations  14.7 us (2%)
    reduce_scatter x1, waiting for transfers between devices, body(): lax.psum_scatter(lax.dot_general(gate, cotangent, (((0,), (0,)), ((), ())...  187 us
    psum x1, waiting for transfers between devices, body(): grad_taps = lax.psum(taps_terms, ('dp', 'context')) * scale_factor  95.7 us
    all_gather x1, waiting for transfers between devices, body(): lax.all_gather(out_proj, 'dp', axis=0, tiled=True)  84.6 us
    reduce_scatter x1, waiting for transfers between devices, body(): lax.psum_scatter(filter_local, 'dp', scatter_dimension=1, tiled=True)  29.9 us
    all_to_all x1, blocking collectives, body(): lax.all_to_all(long_chan.astype(jnp.bfloat16), 'context', split_axis=1, c...  19.9 us
    dot_general x3, matrix products, inverse_real(): undo = jnp.einsum('ckn,nm->ckm', spectrum, inner_back, precision=PRECISE)  14.4 us
    all_to_all x1, waiting for transfers between devices, body(): lax.all_to_all(back_chan.astype(jnp.bfloat16), 'context', split_axis=1, c...  13.4 us
  transfers between devices with their start and end apart: 15, of which 9 were waited for; matrix products, arithmetic and copies ran while one was open for 5% of the time, Pallas kernels for 0%

profile of v1, /device:TPU:0, one launch (start us, length us, event | category | flops | bytes accessed | tf_op | source)
XLA Modules:
  0.0 624.0 jit_solution(17891902546666349391)
XLA Ops:
  7.9 0.9 slice.124
  8.8 2.4 collective-permute-start
  11.2 1.1 fusion.102
  12.9 1.7 copy-done.1
  14.6 1.0 add_convert_fusion
  15.6 84.6 %all-gather.2.cloned.1.call-done = bf16[2048,2048]{1,0:T(8,128)(2,1)} async-done(((bf16[512,2048]{1,0:T(8,128)(2,1)}), bf16[2048,2048]{1,0:T(8,128)(2,1)}) %all-gather.2.cloned.1.call-update) | async-done | bytes 8388624 | tf_op jit(solution)/shard_map/all_gather | solution.py:124
  100.2 6.3 %fusion.21 = f32[128,2048]{1,0:T(8,128)S(1)} fusion(bf16[128,2048]{1,0:T(8,128)(2,1)S(1)} %copy-done, bf16[2048,2048]{1,0:T(8,128)(2,1)} %all-gather.2.cloned.1.call-done), kind=kOutput, calls=%fused_computation.36 | convolution fusion | flops 1074266112 | bytes 9961472 | tf_op jit(solution)/shard_map/dot_general | solution.py:122
  106.5 1.0 copy-done.10
  107.6 1.0 copy.97
  108.6 4.6 all-to-all-start.1
  113.3 1.4 copy.105
  115.5 4.0 convolution_bitcast_fusion.2
  119.6 9.0 %all-to-all-done.1 = bf16[8,256,128]{2,1,0:T(8,128)(2,1)S(1)} async-done(((bf16[8,256,128]{2,1,0:T(8,128)(2,1)}), bf16[8,256,128]{2,1,0:T(8,128)(2,1)S(1)}, u32[]{:S(2)}, u32[]{:S(2)}) %all-to-all-start.1) | async-done | bytes 524320 | tf_op jit(solution)/shard_map/all_to_all | solution.py:138
  128.6 1.4 convolution_bitcast_fusion
  130.8 0.9 multiply_subtract_fusion.8
  132.4 4.2 fusion.16
  136.6 4.2 fusion.12
  140.8 0.9 multiply_add_fusion.3
  141.8 1.0 copy-done.5
  142.8 2.6 pad_maximum_fusion.4
  145.4 5.4 copy.88
  150.8 4.0 fusion.61
  155.5 3.2 fusion.40
  158.7 0.9 copy.78
  159.6 3.5 all-to-all-start.2
  163.6 1.4 copy.103
  165.0 13.4 %all-to-all-done.2 = bf16[256,8,128]{2,0,1:T(8,128)(2,1)S(1)} async-done(((bf16[256,8,128]{2,0,1:T(8,128)(2,1)}), bf16[256,8,128]{2,0,1:T(8,128)(2,1)S(1)}, u32[]{:S(2)}, u32[]{:S(2)}) %all-to-all-start.2) | async-done | bytes 524320 | tf_op jit(solution)/shard_map/all_to_all | solution.py:147
  178.5 1.3 copy.100
  179.8 2.8 convert_multiply_fusion.4
  182.8 1.8 collective-permute-start.3
  184.7 2.5 collective-permute-start.5
  187.3 1.3 collective-permute-start.6
  188.6 2.4 collective-permute-start.7
  191.1 4.5 collective-permute-done.4
  195.5 0.9 collective-permute-done.5
  196.8 1.4 convolution_bitcast_fusion.1
  199.0 4.1 fusion.14
  203.1 4.5 multiply_add_fusion.1
  207.6 4.6 pad_maximum_fusion.2
  212.1 5.7 copy.85
  217.9 6.1 fusion.63
  224.0 2.3 pad_maximum_fusion.5
  226.3 5.5 copy.91
  231.8 4.3 fusion.59
  236.1 2.8 multiply_add_fusion
  238.9 2.2 fusion.37
  241.1 2.5 copy.96
  243.7 1.8 fusion.46
  245.4 19.9 %all_to_all.39 = bf16[256,8,128]{0,2,1:T(8,128)(2,1)S(1)} all-to-all(bf16[256,8,128]{0,2,1:T(8,128)(2,1)S(1)} %bitcast.111), channel_id=1, replica_groups=mesh['dp'=4,'context'=8] {'context'}, dimensions={1} | all-to-all | bytes 1048576 | tf_op jit(solution)/shard_map/all_to_all | solution.py:118
  265.7 0.9 copy-done.9
  266.8 1.3 collective-permute-start.8
  268.1 1.8 collective-permute-done.8
  270.3 1.6 copy-done.2
  271.9 3.0 multiply_reduce_fusion.2
  275.7 3.4 fusion.22
  279.1 1.2 copy.121
  280.6 9.2 %fusion.49 = f32[2048,2048]{1,0:T(8,128)} fusion(bf16[128,2048]{1,0:T(8,128)(2,1)S(1)} %copy-done, f32[2048,128]{0,1:T(8,128)S(1)} %bitcast.105, bf16[128,6144]{1,0:T(8,128)(2,1)} %copy-done.12), kind=kOutput, calls=%fused_computation.82 | convolution fusion | flops 1074528256 | bytes 18874368 | tf_op jit(solution)/shard_map/dot_general | solution.py:129
  289.7 8.9 %psum.15 = f32[256]{0:T(256)S(1)} all-reduce(f32[256]{0:T(256)S(1)} %get-tuple-element.32), channel_id=1, replica_groups=mesh['dp'=4,'context'=8] {'dp'}, use_global_device_ids=true, to_apply=%region_6.7 | all-reduce | flops 256 | bytes 2048 | tf_op jit(solution)/shard_map/psum | solution.py:154
  299.3 95.7 %all-reduce.2.cloned.1.call-done = f32[3,6144]{1,0:T(4,128)} async-done(((f32[3,6144]{1,0:T(4,128)}), f32[3,6144]{1,0:T(4,128)}) %all-reduce.2.cloned.1.call-update) | async-done | bytes 73744 | tf_op jit(solution)/shard_map/psum | solution.py:172
  394.9 1.6 broadcast_multiply_fusion.2
  396.5 29.9 %reduce-scatter.3.cloned.1.call-done = f32[256,256]{1,0:T(8,128)} async-done(((f32[256,1024]{1,0:T(8,128)}), f32[256,256]{1,0:T(8,128)}) %reduce-scatter.3.cloned.1.call-update) | async-done | bytes 262160 | tf_op jit(solution)/shard_map/reduce_scatter | solution.py:152
  426.4 1.7 broadcast_multiply_fusion.1
  428.1 187.3 %reduce-scatter.5.cloned.1.call-done = f32[64,2048]{1,0:T(8,128)} async-done(((f32[2048,2048]{1,0:T(8,128)}), f32[64,2048]{1,0:T(8,128)}) %reduce-scatter.5.cloned.1.call-update) | async-done | bytes 524304 | tf_op jit(solution)/shard_map/reduce_scatter | solution.py:128
  615.4 1.9 broadcast_multiply_fusion
  (88 shorter events, 9.0 us)
Async XLA Ops:
  7.2 93.1 %copy-start = (bf16[128,2048]{1,0:T(8,128)(2,1)S(1)}, bf16[128,2048]{1,0:T(8,128)(2,1)}, u32[]{:S(2)}) copy-start(bf16[128,2048]{1,0:T(8,128)(2,1)} %param.11) | copy-start | bytes 1572868
  7.2 5.2 copy-start.17
  7.2 93.0 %all-gather.2.cloned.1.call-start = ((), (), s32[]{:S(2)}) async-start(), calls=%async_computation.5 | async-start | bytes 10485760 | tf_op jit(solution)/shard_map/all_gather | solution.py:124
  8.8 3.6 collective-permute-start
  12.9 1.7 copy-start.1
  15.6 90.9 %copy-start.12 = (bf16[128,6144]{1,0:T(8,128)(2,1)}, bf16[128,6144]{1,0:T(8,128)(2,1)S(1)}, u32[]{:S(2)}) copy-start(bf16[128,6144]{1,0:T(8,128)(2,1)S(1)} %add_convert_fusion) | copy-start | bytes 4718596
  106.5 1.0 copy-start.10
  108.6 20.0 %all-to-all-start.1 = ((bf16[8,256,128]{2,1,0:T(8,128)(2,1)}), bf16[8,256,128]{2,1,0:T(8,128)(2,1)S(1)}, u32[]{:S(2)}, u32[]{:S(2)}) async-start(bf16[8,256,128]{2,1,0:T(8,128)(2,1)} %bitcast.24), calls=%async_computation.1 | async-start | bytes 1048576 | tf_op jit(solution)/shard_map/all_to_all | solution.py:138
  128.6 2.2 copy-start.7
  136.6 4.2 copy-start.3
  140.8 2.0 copy-start.5
  154.9 0.7 copy-start.18
  159.6 18.8 %all-to-all-start.2 = ((bf16[256,8,128]{2,0,1:T(8,128)(2,1)}), bf16[256,8,128]{2,0,1:T(8,128)(2,1)S(1)}, u32[]{:S(2)}, u32[]{:S(2)}) async-start(bf16[256,8,128]{2,0,1:T(8,128)(2,1)} %copy.78), calls=%async_computation.2 | async-start | bytes 1048576 | tf_op jit(solution)/shard_map/all_to_all | solution.py:147
  163.1 231.8 %all-reduce.2.cloned.1.call-start = ((), (), s32[]{:S(2)}) async-start(), calls=%async_computation.6 | async-start | bytes 196608 | tf_op jit(solution)/shard_map/psum | solution.py:172
  182.6 4.6 collective-permute-start.1
  182.7 5.9 collective-permute-start.2
  182.8 8.2 %collective-permute-start.3 = (bf16[256,128]{0,1:T(8,128)(2,1)S(1)}, bf16[256,128]{0,1:T(8,128)(2,1)S(1)}, u32[]{:S(2)}, u32[]{:S(2)}) collective-permute-start(bf16[256,128]{0,1:T(8,128)(2,1)S(1)} %get-tuple-element.38), channel_id=1, source_target_pairs={{0,3},{1,2},{2,1},{3,0},{4,7},{5,6},{6,5},{7,4},{8,11},{9,10},{10,... | collective-permute-start | bytes 196616 | tf_op jit(solution)/shard_map/ppermute | solution.py:106
  184.6 11.0 %collective-permute-start.4 = (bf16[256,128]{0,1:T(8,128)(2,1)S(1)}, bf16[256,128]{0,1:T(8,128)(2,1)S(1)}, u32[]{:S(2)}, u32[]{:S(2)}) collective-permute-start(bf16[256,128]{0,1:T(8,128)(2,1)S(1)} %get-tuple-element.37), channel_id=1, source_target_pairs={{0,4},{1,5},{2,6},{3,7},{4,0},{5,1},{6,2},{7,3},{8,12},{9,13},{10,... | collective-permute-start | bytes 196616 | tf_op jit(solution)/shard_map/ppermute | solution.py:106
  184.7 11.7 %collective-permute-start.5 = (bf16[256,128]{0,1:T(8,128)(2,1)S(1)}, bf16[256,128]{0,1:T(8,128)(2,1)S(1)}, u32[]{:S(2)}, u32[]{:S(2)}) collective-permute-start(bf16[256,128]{0,1:T(8,128)(2,1)S(1)} %get-tuple-element.36), channel_id=1, source_target_pairs={{0,5},{1,4},{2,7},{3,6},{4,1},{5,0},{6,3},{7,2},{8,13},{9,12},{10,... | collective-permute-start | bytes 196616 | tf_op jit(solution)/shard_map/ppermute | solution.py:106
  187.3 9.2 %collective-permute-start.6 = (bf16[256,128]{0,1:T(8,128)(2,1)S(1)}, bf16[256,128]{0,1:T(8,128)(2,1)S(1)}, u32[]{:S(2)}, u32[]{:S(2)}) collective-permute-start(bf16[256,128]{0,1:T(8,128)(2,1)S(1)} %get-tuple-element.35), channel_id=1, source_target_pairs={{0,6},{1,7},{2,4},{3,5},{4,2},{5,3},{6,0},{7,1},{8,14},{9,15},{10,... | collective-permute-start | bytes 196616 | tf_op jit(solution)/shard_map/ppermute | solution.py:106
  188.6 7.9 %collective-permute-start.7 = (bf16[256,128]{0,1:T(8,128)(2,1)S(1)}, bf16[256,128]{0,1:T(8,128)(2,1)S(1)}, u32[]{:S(2)}, u32[]{:S(2)}) collective-permute-start(bf16[256,128]{0,1:T(8,128)(2,1)S(1)} %get-tuple-element.34), channel_id=1, source_target_pairs={{0,7},{1,6},{2,5},{3,4},{4,3},{5,2},{6,1},{7,0},{8,15},{9,14},{10,... | collective-permute-start | bytes 196616 | tf_op jit(solution)/shard_map/ppermute | solution.py:106
  196.5 2.1 copy-start.15
  199.0 4.1 copy-start.4
  199.0 4.1 copy-start.6
  217.9 6.1 copy-start.13
  217.9 6.1 copy-start.14
  231.8 4.3 copy-start.8
  238.9 4.8 copy-start.16
  245.4 20.1 %copy-start.11 = (f32[128,2048]{1,0:T(8,128)S(1)}, f32[128,2048]{1,0:T(8,128)}, u32[]{:S(2)}) copy-start(f32[128,2048]{1,0:T(8,128)} %copy-done.10) | copy-start | bytes 3145732
  265.3 1.2 copy-start.9
  266.8 3.1 collective-permute-start.8
  269.9 1.9 copy-start.2
  275.6 150.8 %reduce-scatter.3.cloned.1.call-start = ((), (), s32[]{:S(2)}) async-start(), calls=%async_computation.7 | async-start | bytes 1310720 | tf_op jit(solution)/shard_map/reduce_scatter | solution.py:152
  280.3 335.1 %reduce-scatter.5.cloned.1.call-start = ((), (), s32[]{:S(2)}) async-start(), calls=%async_computation.8 | async-start | bytes 17301504 | tf_op jit(solution)/shard_map/reduce_scatter | solution.py:128
Sparse Core Ops, SparseCore 0:
  9.9 90.2 all-gather.1
  275.7 119.1 all-reduce.1
  397.8 28.5 reduce-scatter.2
  428.7 186.6 reduce-scatter.4
